TPU v7x, 512 devices: a whole 4x4x16 slice. The times are simulated.
512 devices in a mesh: blk: 32 (over y, x, core), mpo: 16 (over z).
Axes of the slice: x: 4, y: 4, z: 16, core: 2. Of those that a mesh axis runs over, the one named last changes fastest.
Arguments:
- theta: float32 [64, 128, 16, 128], P('blk'), may hold values from -6 to 6
- block_dims: int32 [64, 2], P('blk'), may hold values from 32 to 128, as said below
- pair_mask: int32 [96, 64], P(None, 'blk'), may hold values 0 or 1
- term_charge: int32 [96], replicated, may hold values from -1 to 1
- left_env: float32 [96, 64, 128, 128], P('mpo', 'blk'), may hold values from -0.5 to 0.5
- right_env: float32 [96, 64, 128, 128], P('mpo', 'blk'), may hold values from -0.5 to 0.5
- site_one: float32 [96, 4, 4], replicated, may hold values from -0.3125 to 0.3125
- site_two: float32 [96, 4, 4], replicated, may hold values from -3 to 3
Outputs:
- hpsi: float32 [64, 128, 16, 128], P('blk', 'mpo')
Inputs may be any that keep to these rules, and one draw needn't show every extreme that they name: `block_dims`: kept dimensions of each sector; rows and columns of a block beyond them are empty. The first sector keeps 128 on both sides.
All inputs are finite; a program needn't handle non-finite values. No bound on the sum of `pair_mask` on one device may be relied on, other than what follows from the above.
Results may differ from a plain program's by a relative error of at most 0.0003.
Values sent between devices are 32-bit elements; how exact they have to be, the bound alone decides.
A program may use at most 64 MiB of HBM per device.

v0:
```python
import jax
import jax.numpy as jnp
from jax import lax
from jax.sharding import PartitionSpec as P


def extended(cells, sides, width):
    for axis, dim in sides:
        count = lax.axis_size(axis)
        ends = count - 1
        head = lax.slice_in_dim(cells, 0, width, axis=dim)
        tail = lax.slice_in_dim(cells, cells.shape[dim] - width, cells.shape[dim], axis=dim)
        cells = jnp.concatenate(
            [
                lax.ppermute(tail, axis, [(i, (i + 1) % count) for i in range(ends)]),
                cells,
                lax.ppermute(head, axis, [((i + 1) % count, i) for i in range(ends)]),
            ],
            axis=dim,
        )
    return cells


def sector_mask(block_dims, bond_cap):
    positions = jnp.arange(bond_cap, dtype=jnp.int32)
    left_ok = positions[None, :] < block_dims[:, 0:1]
    right_ok = positions[None, :] < block_dims[:, 1:2]
    return (left_ok[:, :, None] & right_ok[:, None, :]).astype(jnp.float32)


def make_pair(first_op, second_op):
    states = first_op.shape[0]
    return (first_op[:, None, :, None] * second_op[None, :, None, :]).reshape(
        states * states, states * states
    )


def apply_term(left_rows, source, site_pair, right_block):
    highest = lax.Precision.HIGHEST
    row_count = left_rows.shape[0]
    moved = jnp.dot(
        left_rows,
        source.reshape(source.shape[0], -1),
        precision=highest,
        preferred_element_type=jnp.float32,
    )
    moved = moved.reshape(row_count, source.shape[1], source.shape[2])
    mixed = jnp.einsum("pq,aqd->apd", site_pair, moved, precision=highest)
    return jnp.einsum("apd,bd->apb", mixed, right_block, precision=highest)


def all_sectors(running, padded, left_all, right_all, charge, site_pair, allowed):
    sectors = left_all.shape[0]
    source_index = jnp.arange(sectors, dtype=jnp.int32) + 1 - charge

    def per_sector(left_rows, index, right_block):
        source = lax.dynamic_index_in_dim(padded, index, 0, keepdims=False)
        return apply_term(left_rows, source, site_pair, right_block)

    terms = jax.vmap(per_sector)(left_all, source_index, right_all)
    return running + allowed.astype(jnp.float32)[:, None, None, None] * terms


def body(theta, block_dims, pair_mask, term_charge, left_env, right_env, site_one, site_two):
    bond_cap = theta.shape[1]
    group_index = lax.axis_index("mpo")
    group_count = lax.axis_size("mpo")
    row_count = bond_cap // group_count
    first_row = group_index * row_count
    block_mask = sector_mask(block_dims, bond_cap)
    masked = theta * block_mask[:, :, None, :]
    padded = extended(masked, (("blk", 0),), 1)
    row_mask = lax.dynamic_slice_in_dim(block_mask, first_row, row_count, 1)
    term_count = left_env.shape[0]
    first_term = group_index * term_count

    def local_term(w, running):
        term_index = first_term + w
        charge = lax.dynamic_index_in_dim(term_charge, term_index, 0, keepdims=False)
        allowed = lax.dynamic_index_in_dim(pair_mask, term_index, 0, keepdims=False)
        first_op = lax.dynamic_index_in_dim(site_one, term_index, 0, keepdims=False)
        second_op = lax.dynamic_index_in_dim(site_two, term_index, 0, keepdims=False)
        left_all = lax.dynamic_index_in_dim(left_env, w, 0, keepdims=False)
        right_all = lax.dynamic_index_in_dim(right_env, w, 0, keepdims=False)
        return all_sectors(
            running, padded, left_all, right_all, charge, make_pair(first_op, second_op), allowed
        )

    partial_value = lax.fori_loop(0, term_count, local_term, jnp.zeros(theta.shape, jnp.float32))
    whole_sum = lax.psum(partial_value, "mpo")
    mine = lax.dynamic_slice_in_dim(whole_sum, first_row, row_count, 1)
    return mine * row_mask[:, :, None, :]


def solution(mesh):
    placed = (
        P("blk", None, None, None),
        P("blk", None),
        P(None, "blk"),
        P(),
        P("mpo", "blk", None, None),
        P("mpo", "blk", None, None),
        P(),
        P(),
    )
    return jax.shard_map(
        body, mesh=mesh, in_specs=placed, out_specs=P("blk", "mpo", None, None), check_vma=False
    )
```

profile of v0, /device:TPU:2, one launch (start us, length us, event | category | flops | bytes accessed | tf_op | source)
XLA Modules:
  0.0 307.2 jit_solution(4016067030616916532)
XLA Ops:
  6.5 1.0 slice_reduce_fusion.1
  7.7 2.2 copy_multiply_fusion
  10.0 1.2 fusion.20
  11.1 1.9 collective-permute-start
  13.1 3.6 %collective-permute-start.1 = (f32[1,128,16,128]{3,1,2,0:T(8,128)S(1)}, f32[1,128,16,128]{3,1,2,0:T(8,128)}, u32[]{:S(2)}, u32[]{:S(2)}) collective-permute-start(f32[1,128,16,128]{3,1,2,0:T(8,128)S(1)} %get-tuple-element.253), channel_id=1, source_target_pairs={{16,0},{32,16},{48,32},{64,48},{80,64},{96,80},{112,96},{128,112},... | collective-permute-start | bytes 3145736 | tf_op jit(solution)/shard_map/ppermute | solution.py:17
  17.8 9.7 %collective-permute-done = f32[1,128,16,128]{3,1,2,0:T(8,128)} collective-permute-done((f32[1,128,16,128]{3,1,2,0:T(8,128)}, f32[1,128,16,128]{3,1,2,0:T(8,128)}, u32[]{:S(2)}, u32[]{:S(2)}) %collective-permute-start) | collective-permute-done | bytes 1048608 | tf_op jit(solution)/shard_map/ppermute | solution.py:15
  27.6 1.4 collective-permute-done.1
  29.0 4.0 %pad_maximum_fusion = f32[4,128,16,128]{3,1,2,0:T(8,128)} fusion(f32[1,128,16,128]{3,1,2,0:T(8,128)} %collective-permute-done.1, f32[2,128,16,128]{3,1,2,0:T(8,128)S(1)} %copy_multiply_fusion, f32[1,128,16,128]{3,1,2,0:T(8,128)} %collective-permute-done), kind=kLoop, calls=%fused_computation.25 | loop fusion | flops 2097152 | bytes 8388608 | tf_op jit(solution)/shard_map/concatenate | solution.py:13
  33.0 109.8 %while.14 = (s32[]{:T(128)}, f32[2,128,16,128]{3,1,2,0:T(8,128)}, s32[]{:T(128)}, s32[96,2]{1,0:T(8,128)S(1)}, f32[6,2,128,128]{3,2,1,0:T(8,128)}, /*index=5*/s3...) while((s32[]{:T(128)}, f32[2,128,16,128]{3,1,2,0:T(8,128)}, ...), condition=%wide.region_1.2_spmd.clone, body=%wide.region_0.1_spmd.clone.sunk | while | flops 1712849152 | bytes 44307156 | solution.py:89
  35.0 2.9 gather_fusion
  37.8 1.9 copy.37
  39.7 3.6 %fusion.37 = f32[2,128,2048]{2,1,0:T(8,128)S(1)} fusion(f32[2,128,2048]{1,2,0:T(8,128)} %bitcast.61, f32[6,2,128,128]{3,2,1,0:T(8,128)} %get-tuple-element.351, s32[]{:T(128)S(6)} %copy.41), kind=kOutput, calls=%fused_computation.8.clone.1 | convolution fusion | flops 805306368 | bytes 4325380 | tf_op jit(solution)/shard_map/while/body/eval_jaxpr/vmap()/dot_general | solution.py:41
  43.7 1.9 fusion.38
  45.6 4.4 %select_add_fusion.2 = f32[2,128,16,128]{3,1,2,0:T(8,128)S(1)} fusion(f32[2,128,16,128]{3,1,2,0:T(8,128)S(1)} %copy-done, f32[2,128,128,16]{2,3,1,0:T(8,128)S(1)} %fusion.38, f32[2]{0:T(128)S(1)} %fusion.39, pred[]{:T(512)S(6)} %compare.3, f32[6,2,128,128]{3,2,1,0:T(8,128)} %get-tuple-element.356, s32[]{:T(128)S(6)} %copy.41), kind=kOutput, calls=%fused_computation.6.clone.1 | convolution fusion | flops 806879232 | bytes 6422541 | tf_op jit(solution)/shard_map/while/body/eval_jaxpr/vmap(apd,bd->apb)/dot_general | solution.py:49
  50.0 1.3 copy-done.1
  53.3 2.9 gather_fusion
  56.1 1.9 copy.37
  58.0 3.6 %fusion.37 = f32[2,128,2048]{2,1,0:T(8,128)S(1)} fusion(f32[2,128,2048]{1,2,0:T(8,128)} %bitcast.61, f32[6,2,128,128]{3,2,1,0:T(8,128)} %get-tuple-element.351, s32[]{:T(128)S(6)} %copy.41), kind=kOutput, calls=%fused_computation.8.clone.1 | convolution fusion | flops 805306368 | bytes 4325380 | tf_op jit(solution)/shard_map/while/body/eval_jaxpr/vmap()/dot_general | solution.py:41
  62.0 1.9 fusion.38
  63.9 4.4 %select_add_fusion.2 = f32[2,128,16,128]{3,1,2,0:T(8,128)S(1)} fusion(f32[2,128,16,128]{3,1,2,0:T(8,128)S(1)} %copy-done, f32[2,128,128,16]{2,3,1,0:T(8,128)S(1)} %fusion.38, f32[2]{0:T(128)S(1)} %fusion.39, pred[]{:T(512)S(6)} %compare.3, f32[6,2,128,128]{3,2,1,0:T(8,128)} %get-tuple-element.356, s32[]{:T(128)S(6)} %copy.41), kind=kOutput, calls=%fused_computation.6.clone.1 | convolution fusion | flops 806879232 | bytes 6422541 | tf_op jit(solution)/shard_map/while/body/eval_jaxpr/vmap(apd,bd->apb)/dot_general | solution.py:49
  68.3 1.3 copy-done.1
  71.6 2.9 gather_fusion
  74.4 1.9 copy.37
  76.3 3.6 %fusion.37 = f32[2,128,2048]{2,1,0:T(8,128)S(1)} fusion(f32[2,128,2048]{1,2,0:T(8,128)} %bitcast.61, f32[6,2,128,128]{3,2,1,0:T(8,128)} %get-tuple-element.351, s32[]{:T(128)S(6)} %copy.41), kind=kOutput, calls=%fused_computation.8.clone.1 | convolution fusion | flops 805306368 | bytes 4325380 | tf_op jit(solution)/shard_map/while/body/eval_jaxpr/vmap()/dot_general | solution.py:41
  80.3 1.9 fusion.38
  82.2 4.4 %select_add_fusion.2 = f32[2,128,16,128]{3,1,2,0:T(8,128)S(1)} fusion(f32[2,128,16,128]{3,1,2,0:T(8,128)S(1)} %copy-done, f32[2,128,128,16]{2,3,1,0:T(8,128)S(1)} %fusion.38, f32[2]{0:T(128)S(1)} %fusion.39, pred[]{:T(512)S(6)} %compare.3, f32[6,2,128,128]{3,2,1,0:T(8,128)} %get-tuple-element.356, s32[]{:T(128)S(6)} %copy.41), kind=kOutput, calls=%fused_computation.6.clone.1 | convolution fusion | flops 806879232 | bytes 6422541 | tf_op jit(solution)/shard_map/while/body/eval_jaxpr/vmap(apd,bd->apb)/dot_general | solution.py:49
  86.6 1.3 copy-done.1
  89.9 2.9 gather_fusion
  92.8 1.9 copy.37
  94.6 3.6 %fusion.37 = f32[2,128,2048]{2,1,0:T(8,128)S(1)} fusion(f32[2,128,2048]{1,2,0:T(8,128)} %bitcast.61, f32[6,2,128,128]{3,2,1,0:T(8,128)} %get-tuple-element.351, s32[]{:T(128)S(6)} %copy.41), kind=kOutput, calls=%fused_computation.8.clone.1 | convolution fusion | flops 805306368 | bytes 4325380 | tf_op jit(solution)/shard_map/while/body/eval_jaxpr/vmap()/dot_general | solution.py:41
  98.6 1.9 fusion.38
  100.5 4.4 %select_add_fusion.2 = f32[2,128,16,128]{3,1,2,0:T(8,128)S(1)} fusion(f32[2,128,16,128]{3,1,2,0:T(8,128)S(1)} %copy-done, f32[2,128,128,16]{2,3,1,0:T(8,128)S(1)} %fusion.38, f32[2]{0:T(128)S(1)} %fusion.39, pred[]{:T(512)S(6)} %compare.3, f32[6,2,128,128]{3,2,1,0:T(8,128)} %get-tuple-element.356, s32[]{:T(128)S(6)} %copy.41), kind=kOutput, calls=%fused_computation.6.clone.1 | convolution fusion | flops 806879232 | bytes 6422541 | tf_op jit(solution)/shard_map/while/body/eval_jaxpr/vmap(apd,bd->apb)/dot_general | solution.py:49
  104.9 1.3 copy-done.1
  108.2 2.9 gather_fusion
  111.1 1.9 copy.37
  112.9 3.6 %fusion.37 = f32[2,128,2048]{2,1,0:T(8,128)S(1)} fusion(f32[2,128,2048]{1,2,0:T(8,128)} %bitcast.61, f32[6,2,128,128]{3,2,1,0:T(8,128)} %get-tuple-element.351, s32[]{:T(128)S(6)} %copy.41), kind=kOutput, calls=%fused_computation.8.clone.1 | convolution fusion | flops 805306368 | bytes 4325380 | tf_op jit(solution)/shard_map/while/body/eval_jaxpr/vmap()/dot_general | solution.py:41
  116.9 1.9 fusion.38
  118.8 4.4 %select_add_fusion.2 = f32[2,128,16,128]{3,1,2,0:T(8,128)S(1)} fusion(f32[2,128,16,128]{3,1,2,0:T(8,128)S(1)} %copy-done, f32[2,128,128,16]{2,3,1,0:T(8,128)S(1)} %fusion.38, f32[2]{0:T(128)S(1)} %fusion.39, pred[]{:T(512)S(6)} %compare.3, f32[6,2,128,128]{3,2,1,0:T(8,128)} %get-tuple-element.356, s32[]{:T(128)S(6)} %copy.41), kind=kOutput, calls=%fused_computation.6.clone.1 | convolution fusion | flops 806879232 | bytes 6422541 | tf_op jit(solution)/shard_map/while/body/eval_jaxpr/vmap(apd,bd->apb)/dot_general | solution.py:49
  123.2 1.3 copy-done.1
  126.5 2.9 gather_fusion
  129.4 1.9 copy.37
  131.2 3.6 %fusion.37 = f32[2,128,2048]{2,1,0:T(8,128)S(1)} fusion(f32[2,128,2048]{1,2,0:T(8,128)} %bitcast.61, f32[6,2,128,128]{3,2,1,0:T(8,128)} %get-tuple-element.351, s32[]{:T(128)S(6)} %copy.41), kind=kOutput, calls=%fused_computation.8.clone.1 | convolution fusion | flops 805306368 | bytes 4325380 | tf_op jit(solution)/shard_map/while/body/eval_jaxpr/vmap()/dot_general | solution.py:41
  135.2 1.9 fusion.38
  137.1 4.4 %select_add_fusion.2 = f32[2,128,16,128]{3,1,2,0:T(8,128)S(1)} fusion(f32[2,128,16,128]{3,1,2,0:T(8,128)S(1)} %copy-done, f32[2,128,128,16]{2,3,1,0:T(8,128)S(1)} %fusion.38, f32[2]{0:T(128)S(1)} %fusion.39, pred[]{:T(512)S(6)} %compare.3, f32[6,2,128,128]{3,2,1,0:T(8,128)} %get-tuple-element.356, s32[]{:T(128)S(6)} %copy.41), kind=kOutput, calls=%fused_computation.6.clone.1 | convolution fusion | flops 806879232 | bytes 6422541 | tf_op jit(solution)/shard_map/while/body/eval_jaxpr/vmap(apd,bd->apb)/dot_general | solution.py:49
  141.5 1.3 copy-done.1
  142.8 4.2 %copy.20 = f32[2,128,16,128]{3,2,1,0:T(8,128)} copy(f32[2,128,16,128]{3,1,2,0:T(8,128)} %get-tuple-element.174) | data formatting | bytes 4194304 | tf_op jit(solution)/shard_map/while | solution.py:89
  147.0 151.8 %all-reduce.2.cloned.1.call-done = f32[2,128,16,128]{3,2,1,0:T(8,128)} async-done(((f32[2,128,16,128]{3,2,1,0:T(8,128)}), f32[2,128,16,128]{3,2,1,0:T(8,128)}) %all-reduce.2.cloned.1.call-update) | async-done | bytes 2097168 | tf_op jit(solution)/shard_map/psum | solution.py:90
  298.8 1.6 dynamic-slice_multiply_fusion
  (77 shorter events, 15.4 us)
Async XLA Ops:
  6.5 292.3 %all-reduce.2.cloned.1.call-start = ((), (), s32[]{:S(2)}) async-start(), calls=%async_computation | async-start | bytes 4194304 | tf_op jit(solution)/shard_map/psum | solution.py:90
  9.9 6.8 %copy-start.4 = (s32[96,2]{0,1:T(2,128)S(1)}, s32[96,2]{0,1:T(2,128)}, u32[]{:S(2)}) copy-start(s32[96,2]{0,1:T(2,128)} %param.12) | copy-start | bytes 2308
  10.0 6.9 %copy-start.2 = (f32[96,4,4]{0,2,1:T(4,128)S(1)}, f32[96,4,4]{0,2,1:T(4,128)}, u32[]{:S(2)}) copy-start(f32[96,4,4]{0,2,1:T(4,128)} %param.16) | copy-start | bytes 18436
  10.0 7.0 %copy-start.3 = (f32[96,4,4]{0,2,1:T(4,128)S(1)}, f32[96,4,4]{0,2,1:T(4,128)}, u32[]{:S(2)}) copy-start(f32[96,4,4]{0,2,1:T(4,128)} %param.17) | copy-start | bytes 18436
  11.1 16.4 %collective-permute-start = (f32[1,128,16,128]{3,1,2,0:T(8,128)}, f32[1,128,16,128]{3,1,2,0:T(8,128)}, u32[]{:S(2)}, u32[]{:S(2)}) collective-permute-start(f32[1,128,16,128]{3,1,2,0:T(8,128)} %get-tuple-element.252), channel_id=1, source_target_pairs={{0,16},{16,32},{32,48},{48,64},{64,80},{80,96},{96,112},{112,128},... | collective-permute-start | bytes 3145736 | tf_op jit(solution)/shard_map/ppermute | solution.py:15
  13.1 15.9 %collective-permute-start.1 = (f32[1,128,16,128]{3,1,2,0:T(8,128)S(1)}, f32[1,128,16,128]{3,1,2,0:T(8,128)}, u32[]{:S(2)}, u32[]{:S(2)}) collective-permute-start(f32[1,128,16,128]{3,1,2,0:T(8,128)S(1)} %get-tuple-element.253), channel_id=1, source_target_pairs={{16,0},{32,16},{48,32},{64,48},{80,64},{96,80},{112,96},{128,112},... | collective-permute-start | bytes 3145736 | tf_op jit(solution)/shard_map/ppermute | solution.py:17
  17.8 15.1 %copy-start.5 = (s32[96]{0:T(128)S(1)}, s32[96]{0:T(128)}, u32[]{:S(2)}) copy-start(s32[96]{0:T(128)} %param.13) | copy-start | bytes 1156
  43.7 1.9 copy-start
  49.9 1.3 copy-start.1
  62.0 1.9 copy-start
  68.3 1.3 copy-start.1
  80.3 1.9 copy-start
  86.6 1.3 copy-start.1
  98.6 1.9 copy-start
  104.9 1.3 copy-start.1
  116.9 1.9 copy-start
  123.2 1.3 copy-start.1
  135.2 1.9 copy-start
  141.5 1.3 copy-start.1
Sparse Core Ops, SparseCore 0:
  147.1 151.6 all-reduce.1
where the time goes:
time: 308 us; the launch traced here: 307 us
  waiting for transfers between devices  163 us (53%)
  matrix products  58.9 us (19%)
  local copies, waits for them, and re-layouts  53.9 us (18%)
  between operations  13.5 us (4%)
  other arithmetic  11.8 us (4%)
  starting transfers between devices  5.55 us (2%)
    psum x1, waiting for transfers between devices, body(): whole_sum = lax.psum(partial_value, 'mpo')  152 us
    gather x12, local copies, waits for them, and re-layouts, per_sector(): source = lax.dynamic_index_in_dim(padded, index, 0, keepdims=False)  28.4 us
    dot_general x6, matrix products, apply_term(): return jnp.einsum('apd,bd->apb', mixed, right_block, precision=highest)  26.2 us
    dot_general x6, matrix products, apply_term(): jnp.dot(left_rows, source.reshape(source.shape[0], -1), precision=highest...  21.4 us
    dot_general x6, matrix products, apply_term(): mixed = jnp.einsum('pq,aqd->apd', site_pair, moved, precision=highest)  11.3 us
    while x30, local copies, waits for them, and re-layouts  10.3 us
    ppermute x1, waiting for transfers between devices, extended(): lax.ppermute(tail, axis, [(i, (i + 1) % count) for i in range(ends)])  9.72 us
  transfers between devices with their start and end apart: 3, of which 3 were waited for; matrix products, arithmetic and copies ran while one was open for 0% of the time, Pallas kernels for 0%

commit v1 on v0

--- a/solution.py
+++ b/solution.py
@@ -87,7 +87,11 @@
         )
 
     partial_value = lax.fori_loop(0, term_count, local_term, jnp.zeros(theta.shape, jnp.float32))
-    whole_sum = lax.psum(partial_value, "mpo")
+    whole_sum = partial_value
+    for hop in (1, 2, 4, 8):
+        whole_sum = whole_sum + lax.ppermute(
+            whole_sum, "mpo", [(dev, dev ^ hop) for dev in range(16)]
+        )
     mine = lax.dynamic_slice_in_dim(whole_sum, first_row, row_count, 1)
     return mine * row_mask[:, :, None, :]
 

time: 308 us -> 719 us (2.33)
  the two profiles are of different devices: /device:TPU:2 before, /device:TPU:10 now
where the time goes in v1:
time: 719 us; the launch traced here: 718 us
  waiting for transfers between devices  464 us (65%)
  starting transfers between devices  127 us (18%)
  matrix products  59.1 us (8%)
  local copies, waits for them, and re-layouts  53.2 us (7%)
  other arithmetic  14 us (2%)
    ppermute x4, waiting for transfers between devices, body(): lax.ppermute(whole_sum, 'mpo', [(dev, dev ^ hop) for dev in range(16)])  453 us
    ppermute x4, starting transfers between devices, body(): lax.ppermute(whole_sum, 'mpo', [(dev, dev ^ hop) for dev in range(16)])  122 us
    gather x12, local copies, waits for them, and re-layouts, per_sector(): source = lax.dynamic_index_in_dim(padded, index, 0, keepdims=False)  28.4 us
    dot_general x6, matrix products, apply_term(): return jnp.einsum('apd,bd->apb', mixed, right_block, precision=highest)  26.2 us
    dot_general x6, matrix products, apply_term(): jnp.dot(left_rows, source.reshape(source.shape[0], -1), precision=highest...  21.4 us
  transfers between devices with their start and end apart: 6, of which 6 were waited for; matrix products, arithmetic and copies ran while one was open for 0% of the time, Pallas kernels for 0%

profile of v1, /device:TPU:10, one launch (start us, length us, event | category | flops | bytes accessed | tf_op | source)
XLA Modules:
  0.0 718.0 jit_solution(10887411765942785940)
XLA Ops:
  1.2 2.2 copy_multiply_fusion
  4.6 1.9 collective-permute-start
  6.5 3.6 collective-permute-start.1
  11.3 9.7 %collective-permute-done = f32[1,128,16,128]{3,1,2,0:T(8,128)} collective-permute-done((f32[1,128,16,128]{3,1,2,0:T(8,128)}, f32[1,128,16,128]{3,1,2,0:T(8,128)}, u32[]{:S(2)}, u32[]{:S(2)}) %collective-permute-start) | collective-permute-done | bytes 1048608 | tf_op jit(solution)/shard_map/ppermute | solution.py:15
  21.0 1.4 collective-permute-done.1
  22.5 3.9 pad_maximum_fusion
  26.3 111.0 %while.14 = (s32[]{:T(128)}, f32[2,128,16,128]{3,1,2,0:T(8,128)}, s32[]{:T(128)}, s32[96,2]{1,0:T(8,128)S(1)}, f32[6,2,128,128]{3,2,1,0:T(8,128)}, /*index=5*/s3...) while((s32[]{:T(128)}, f32[2,128,16,128]{3,1,2,0:T(8,128)}, ...), condition=%wide.region_1.2_spmd.clone, body=%wide.region_0.1_spmd.clone.sunk | while | flops 1712849152 | bytes 44307156 | solution.py:89
  28.5 2.9 gather_fusion
  31.4 1.9 copy.40
  33.2 3.6 fusion.38
  37.2 1.9 fusion.39
  39.1 4.4 select_add_fusion.2
  47.0 2.9 gather_fusion
  49.9 1.9 copy.40
  51.7 3.6 fusion.38
  55.7 1.9 fusion.39
  57.6 4.4 select_add_fusion.2
  62.0 1.3 copy-done.1
  65.5 2.9 gather_fusion
  68.4 1.9 copy.40
  70.2 3.6 fusion.38
  74.2 1.9 fusion.39
  76.2 4.4 select_add_fusion.2
  84.0 2.9 gather_fusion
  86.9 1.9 copy.40
  88.7 3.6 fusion.38
  92.7 1.9 fusion.39
  94.7 4.4 select_add_fusion.2
  102.5 2.9 gather_fusion
  105.3 1.9 copy.40
  107.2 3.6 fusion.38
  111.2 1.9 fusion.39
  113.1 4.4 select_add_fusion.2
  121.0 2.9 gather_fusion
  123.9 1.9 copy.40
  125.7 3.6 fusion.38
  129.7 1.9 fusion.39
  131.6 4.4 select_add_fusion.2
  137.3 3.0 copy.22
  140.3 4.0 collective-permute-start.2
  144.3 45.3 %collective-permute-done.2 = f32[2,128,16,128]{3,2,1,0:T(8,128)S(1)} collective-permute-done((f32[2,128,16,128]{3,2,1,0:T(8,128)S(1)}, f32[2,128,16,128]{3,2,1,0:T(8,128)S(1)}, u32[]{:S(2)}, u32[]{:S(2)}) %collective-permute-start.2) | collective-permute-done | bytes 2097184 | tf_op jit(solution)/shard_map/ppermute | solution.py:92
  190.8 5.2 collective-permute-start.3
  196.0 91.2 %collective-permute-done.3 = f32[2,128,16,128]{3,2,1,0:T(8,128)S(1)} collective-permute-done((f32[2,128,16,128]{3,2,1,0:T(8,128)S(1)}, f32[2,128,16,128]{3,2,1,0:T(8,128)S(1)}, u32[]{:S(2)}, u32[]{:S(2)}) %collective-permute-start.3) | collective-permute-done | bytes 2097184 | tf_op jit(solution)/shard_map/ppermute | solution.py:92
  287.5 9.2 %collective-permute-start.4 = (f32[2,128,16,128]{3,2,1,0:T(8,128)S(1)}, f32[2,128,16,128]{3,2,1,0:T(8,128)S(1)}, u32[]{:S(2)}, u32[]{:S(2)}) collective-permute-start(f32[2,128,16,128]{3,2,1,0:T(8,128)S(1)} %add.96), channel_id=1, source_target_pairs={{0,4},{1,5},{2,6},{3,7},{4,0},{5,1},{6,2},{7,3},{8,12},{9,13},{10,... | collective-permute-start | bytes 6291464 | tf_op jit(solution)/shard_map/ppermute | solution.py:92
  296.7 225.2 %collective-permute-done.4 = f32[2,128,16,128]{3,2,1,0:T(8,128)S(1)} collective-permute-done((f32[2,128,16,128]{3,2,1,0:T(8,128)S(1)}, f32[2,128,16,128]{3,2,1,0:T(8,128)S(1)}, u32[]{:S(2)}, u32[]{:S(2)}) %collective-permute-start.4) | collective-permute-done | bytes 2097184 | tf_op jit(solution)/shard_map/ppermute | solution.py:92
  522.2 103.1 %collective-permute-start.5 = (f32[2,128,16,128]{3,2,1,0:T(8,128)S(1)}, f32[2,128,16,128]{3,2,1,0:T(8,128)}, u32[]{:S(2)}, u32[]{:S(2)}) collective-permute-start(f32[2,128,16,128]{3,2,1,0:T(8,128)S(1)} %add.97), channel_id=1, source_target_pairs={{0,8},{1,9},{2,10},{3,11},{4,12},{5,13},{6,14},{7,15},{8,0},{9,1},... | collective-permute-start | bytes 6291464 | tf_op jit(solution)/shard_map/ppermute | solution.py:92
  625.3 91.1 %collective-permute-done.5 = f32[2,128,16,128]{3,2,1,0:T(8,128)} collective-permute-done((f32[2,128,16,128]{3,2,1,0:T(8,128)S(1)}, f32[2,128,16,128]{3,2,1,0:T(8,128)}, u32[]{:S(2)}, u32[]{:S(2)}) %collective-permute-start.5) | collective-permute-done | bytes 2097184 | tf_op jit(solution)/shard_map/ppermute | solution.py:92
  716.4 1.6 fusion.20
  (87 shorter events, 26.9 us)
Async XLA Ops:
  3.4 6.8 copy-start.5
  3.4 6.9 copy-start.3
  3.4 7.0 copy-start.4
  4.6 16.4 %collective-permute-start = (f32[1,128,16,128]{3,1,2,0:T(8,128)}, f32[1,128,16,128]{3,1,2,0:T(8,128)}, u32[]{:S(2)}, u32[]{:S(2)}) collective-permute-start(f32[1,128,16,128]{3,1,2,0:T(8,128)} %get-tuple-element.252), channel_id=1, source_target_pairs={{0,16},{16,32},{32,48},{48,64},{64,80},{80,96},{96,112},{112,128},... | collective-permute-start | bytes 3145736 | tf_op jit(solution)/shard_map/ppermute | solution.py:15
  6.5 15.9 %collective-permute-start.1 = (f32[1,128,16,128]{3,1,2,0:T(8,128)S(1)}, f32[1,128,16,128]{3,1,2,0:T(8,128)}, u32[]{:S(2)}, u32[]{:S(2)}) collective-permute-start(f32[1,128,16,128]{3,1,2,0:T(8,128)S(1)} %get-tuple-element.253), channel_id=1, source_target_pairs={{16,0},{32,16},{48,32},{64,48},{80,64},{96,80},{112,96},{128,112},... | collective-permute-start | bytes 3145736 | tf_op jit(solution)/shard_map/ppermute | solution.py:17
  11.3 15.0 %copy-start.6 = (s32[96]{0:T(128)S(1)}, s32[96]{0:T(128)}, u32[]{:S(2)}) copy-start(s32[96]{0:T(128)} %param.13) | copy-start | bytes 1156
  37.2 1.9 copy-start
  43.5 1.3 copy-start.1
  55.7 1.9 copy-start
  62.0 1.3 copy-start.1
  74.2 1.9 copy-start
  80.5 1.3 copy-start.1
  92.7 1.9 copy-start
  99.0 1.3 copy-start.1
  111.2 1.9 copy-start
  117.5 1.3 copy-start.1
  129.7 1.9 copy-start
  136.0 1.3 copy-start.1
  137.3 52.3 %copy-start.2 = (f32[2,128,16,128]{3,1,2,0:T(8,128)S(1)}, f32[2,128,16,128]{3,1,2,0:T(8,128)}, u32[]{:S(2)}) copy-start(f32[2,128,16,128]{3,1,2,0:T(8,128)} %get-tuple-element.174) | copy-start | bytes 6291460
  140.3 49.3 %collective-permute-start.2 = (f32[2,128,16,128]{3,2,1,0:T(8,128)S(1)}, f32[2,128,16,128]{3,2,1,0:T(8,128)S(1)}, u32[]{:S(2)}, u32[]{:S(2)}) collective-permute-start(f32[2,128,16,128]{3,2,1,0:T(8,128)S(1)} %copy.22), channel_id=1, source_target_pairs={{0,1},{1,0},{2,3},{3,2},{4,5},{5,4},{6,7},{7,6},{8,9},{9,8},{10,11... | collective-permute-start | bytes 6291464 | tf_op jit(solution)/shard_map/ppermute | solution.py:92
  190.8 96.4 %collective-permute-start.3 = (f32[2,128,16,128]{3,2,1,0:T(8,128)S(1)}, f32[2,128,16,128]{3,2,1,0:T(8,128)S(1)}, u32[]{:S(2)}, u32[]{:S(2)}) collective-permute-start(f32[2,128,16,128]{3,2,1,0:T(8,128)S(1)} %copy_add_fusion), channel_id=1, source_target_pairs={{0,2},{1,3},{2,0},{3,1},{4,6},{5,7},{6,4},{7,5},{8,10},{9,11},{10,... | collective-permute-start | bytes 6291464 | tf_op jit(solution)/shard_map/ppermute | solution.py:92
  287.5 234.4 %collective-permute-start.4 = (f32[2,128,16,128]{3,2,1,0:T(8,128)S(1)}, f32[2,128,16,128]{3,2,1,0:T(8,128)S(1)}, u32[]{:S(2)}, u32[]{:S(2)}) collective-permute-start(f32[2,128,16,128]{3,2,1,0:T(8,128)S(1)} %add.96), channel_id=1, source_target_pairs={{0,4},{1,5},{2,6},{3,7},{4,0},{5,1},{6,2},{7,3},{8,12},{9,13},{10,... | collective-permute-start | bytes 6291464 | tf_op jit(solution)/shard_map/ppermute | solution.py:92
  522.2 194.2 %collective-permute-start.5 = (f32[2,128,16,128]{3,2,1,0:T(8,128)S(1)}, f32[2,128,16,128]{3,2,1,0:T(8,128)}, u32[]{:S(2)}, u32[]{:S(2)}) collective-permute-start(f32[2,128,16,128]{3,2,1,0:T(8,128)S(1)} %add.97), channel_id=1, source_target_pairs={{0,8},{1,9},{2,10},{3,11},{4,12},{5,13},{6,14},{7,15},{8,0},{9,1},... | collective-permute-start | bytes 6291464 | tf_op jit(solution)/shard_map/ppermute | solution.py:92
